TPU v7x, 128 devices: a whole 4x4x4 slice. The times are simulated.
128 devices in a mesh: row: 8 (over y, core), col: 16 (over x, z).
Axes of the slice: x: 4, y: 4, z: 4, core: 2. Of those that a mesh axis runs over, the one named last changes fastest.
Arguments:
- tokens: bfloat16 [1024, 8192], P('row', 'col'), may hold values from -6 to 6
- gate_weight: bfloat16 [8192, 28672], P('col', 'row'), may hold values from -0.09375 to 0.09375
- up_weight: bfloat16 [8192, 28672], P('col', 'row'), may hold values from -0.09375 to 0.09375
- down_weight: bfloat16 [28672, 8192], P('row', 'col'), may hold values from -0.046875 to 0.046875
- gate_mask: int32 [64, 224], P('col', 'row'), may hold values 0 or 1
- up_mask: int32 [64, 224], P('col', 'row'), may hold values 0 or 1
- down_mask: int32 [224, 64], P('row', 'col'), may hold values 0 or 1
Outputs:
- mixed_out: bfloat16 [1024, 8192], P('row', 'col')
Inputs may be any that keep to these rules, and one draw needn't show every extreme that they name: `gate_mask`: each entry keeps (1) or drops (0) one block. `up_mask`: each entry keeps (1) or drops (0) one block. `down_mask`: each entry keeps (1) or drops (0) one block.
All inputs are finite; a program needn't handle non-finite values.
Results may differ from a plain program's by a relative error of at most 0.025.
Values may be sent and summed in bfloat16 or wider, within the bound.
A program may use at most 128 MiB of HBM per device.

v0:
```python
import jax
import jax.numpy as jnp
from jax import lax
from jax.sharding import PartitionSpec as P


def expand(weight, block_mask):
    row_count, col_count = weight.shape
    mask_rows, mask_cols = block_mask.shape
    shaped = weight.reshape(mask_rows, row_count // mask_rows, mask_cols, col_count // mask_cols)
    kept_blocks = shaped * block_mask.astype(weight.dtype)[:, None, :, None]
    return kept_blocks.reshape(row_count, col_count)


def per_device(tokens, gate_weight, up_weight, down_weight, gate_mask, up_mask, down_mask):
    kept_gate = expand(gate_weight, gate_mask)
    kept_up = expand(up_weight, up_mask)
    kept_down = expand(down_weight, down_mask)
    gathered = lax.all_gather(tokens, "row", axis=0, tiled=True)
    gate_part = jnp.dot(gathered, kept_gate, preferred_element_type=jnp.float32)
    up_part = jnp.dot(gathered, kept_up, preferred_element_type=jnp.float32)
    gate_sum, up_sum = (
        lax.psum(gate_part.astype(jnp.bfloat16), "col").astype(jnp.float32),
        lax.psum(up_part.astype(jnp.bfloat16), "col").astype(jnp.float32),
    )
    hidden = (jax.nn.silu(gate_sum) * up_sum).astype(jnp.bfloat16)
    return lax.psum_scatter(
        jnp.dot(hidden, kept_down, preferred_element_type=jnp.float32).astype(jnp.bfloat16),
        "row",
        scatter_dimension=0,
        tiled=True,
    )


def solution(mesh):
    return jax.shard_map(
        per_device,
        mesh=mesh,
        in_specs=(
            P("row", "col"),
            P("col", "row"),
            P("col", "row"),
            P("row", "col"),
            P("col", "row"),
            P("col", "row"),
            P("row", "col"),
        ),
        out_specs=P("row", "col"),
        check_vma=False,
    )
```

profile of v0, /device:TPU:0, one launch (start us, length us, event | category | flops | bytes accessed | tf_op | source)
XLA Modules:
  0.0 304.0 jit_solution(16321837674155461157)
XLA Ops:
  6.5 0.0 all-gather.2.cloned.1.call-start
  6.5 0.7 all-gather.2.cloned.1.call-update
  7.3 0.0 all-reduce.3.cloned.1.call-start
  7.3 0.7 convert_element_type.33
  8.0 0.1 copy.9
  8.1 0.0 copy-start.2
  8.1 6.0 %copy.10 = bf16[512,3584]{0,1:T(8,128)(2,1)} copy(bf16[512,3584]{1,0:T(8,128)(2,1)} %param.8) | data formatting | bytes 7340032 | tf_op args[1]
  14.1 0.0 copy-done.2
  14.1 0.1 copy.11
  14.2 5.9 %copy.12 = bf16[512,3584]{0,1:T(8,128)(2,1)} copy(bf16[512,3584]{1,0:T(8,128)(2,1)} %param.9) | data formatting | bytes 7340032 | tf_op args[2]
  20.1 14.7 %all-gather.2.cloned.1.call-done = bf16[1024,512]{1,0:T(8,128)(2,1)} async-done(((bf16[128,512]{1,0:T(8,128)(2,1)}), bf16[1024,512]{1,0:T(8,128)(2,1)}) %all-gather.2.cloned.1.call-update) | async-done | bytes 1048592 | tf_op jit(solution)/shard_map/all_gather | solution.py:19
  34.8 0.0 copy-start.1
  34.8 1.0 mul.40
  35.8 1.0 copy-done.1
  36.9 0.0 copy-start.5
  36.9 7.4 %fusion.7 = bf16[1024,3584]{0,1:T(8,128)(2,1)} fusion(bf16[1024,512]{1,0:T(8,128)(2,1)} %all-gather.2.cloned.1.call-done, bf16[512,3584]{0,1:T(8,128)(2,1)S(1)} %copy-done.1, bf16[448,8,4,128]{3,2,1,0:T(4,128)(2,1)S(1)} %bitcast.29), kind=kOutput, calls=%fused_computation.10 | convolution fusion | flops 3763601408 | bytes 15728640 | tf_op jit(solution)/shard_map/dot_general | solution.py:20
  44.3 0.0 copy-start
  44.3 1.0 mul.44
  45.3 0.0 copy-done.5
  45.3 1.0 copy-done
  46.4 6.1 %fusion.8 = bf16[1024,3584]{0,1:T(8,128)(2,1)} fusion(bf16[1024,512]{1,0:T(8,128)(2,1)S(1)} %copy-done.5, bf16[512,3584]{0,1:T(8,128)(2,1)S(1)} %copy-done, bf16[448,8,4,128]{3,2,1,0:T(4,128)(2,1)S(1)} %bitcast.27), kind=kOutput, calls=%fused_computation.11 | convolution fusion | flops 3763601408 | bytes 15728640 | tf_op jit(solution)/shard_map/dot_general | solution.py:21
  52.4 0.0 copy-start.3
  52.4 0.0 all-reduce.3.cloned.1.call-update
  52.5 0.0 reduce-scatter.2.cloned.1.call-start
  52.5 0.6 copy-done.3
  53.1 0.1 copy.13
  53.2 198.4 %all-reduce.3.cloned.1.call-done = (bf16[1024,3584]{0,1:T(8,128)(2,1)}, bf16[1024,3584]{0,1:T(8,128)(2,1)}) async-done(((bf16[1024,3584]{0,1:T(8,128)(2,1)}, bf16[1024,3584]{0,1:T(8,128)(2,1)}), (bf16[1024,3584]{0,1:T(8,128)(2,1)}, bf16[1024,3584]{0,1:T(8,128)(2,1)})) %all-reduce.3.cloned.1.call-update) | async-done | bytes 14680080 | tf_op jit(solution)/shard_map/psum | solution.py:24
  251.6 0.0 copy-start.4
  251.6 1.0 mul.48
  252.7 1.0 copy-done.4
  253.7 11.6 %fusion.12 = bf16[1024,512]{1,0:T(8,128)(2,1)} fusion(bf16[3584,512]{1,0:T(8,128)(2,1)S(1)} %copy-done.4, bf16[448,8,4,128]{3,2,1,0:T(4,128)(2,1)S(1)} %bitcast.28, bf16[1024,3584]{0,1:T(8,128)(2,1)} %get-tuple-element.5, bf16[1024,3584]{0,1:T(8,128)(2,1)} %get-tuple-element.6), kind=kOutput, calls=%fused_computation.18 | convolution fusion | flops 3789815808 | bytes 23068672 | tf_op jit(solution)/shard_map/dot_general | solution.py:28
  265.3 0.0 reduce-scatter.2.cloned.1.call-update
  265.3 32.1 %reduce-scatter.2.cloned.1.call-done = bf16[128,512]{1,0:T(8,128)(2,1)} async-done(((bf16[1024,512]{1,0:T(8,128)(2,1)}), bf16[128,512]{1,0:T(8,128)(2,1)}) %reduce-scatter.2.cloned.1.call-update) | async-done | bytes 131088 | tf_op jit(solution)/shard_map/reduce_scatter | solution.py:27
  (2 shorter events, 0.0 us)
Async XLA Ops:
  6.5 28.3 %all-gather.2.cloned.1.call-start = ((), (), s32[]{:S(2)}) async-start(), calls=%async_computation.1 | async-start | bytes 1179648 | tf_op jit(solution)/shard_map/all_gather | solution.py:19
  7.3 244.4 %all-reduce.3.cloned.1.call-start = ((), (), s32[]{:S(2)}) async-start(), calls=%async_computation.3 | async-start | bytes 29360128 | tf_op jit(solution)/shard_map/psum | solution.py:24
  8.1 6.0 %copy-start.2 = (s32[4,28]{1,0:T(4,128)S(1)}, s32[4,28]{1,0:T(4,128)}, u32[]{:S(2)}) copy-start(s32[4,28]{1,0:T(4,128)} %param.12) | copy-start | bytes 1348
  34.8 2.0 copy-start.1
  36.9 8.5 %copy-start.5 = (bf16[1024,512]{1,0:T(8,128)(2,1)S(1)}, bf16[1024,512]{1,0:T(8,128)(2,1)}, u32[]{:S(2)}) copy-start(bf16[1024,512]{1,0:T(8,128)(2,1)} %all-gather.2.cloned.1.call-done) | copy-start | bytes 3145732
  44.3 2.0 copy-start
  52.4 0.7 copy-start.3
  52.5 245.0 %reduce-scatter.2.cloned.1.call-start = ((), (), s32[]{:S(2)}) async-start(), calls=%async_computation.2 | async-start | bytes 1179648 | tf_op jit(solution)/shard_map/reduce_scatter | solution.py:27
  251.6 2.0 copy-start.4
Sparse Core Ops, SparseCore 0:
  9.0 25.7 all-gather.1
  52.6 199.0 all-reduce.2
  265.4 31.9 reduce-scatter.1
where the time goes:
time: 304 us
  waiting for transfers between devices  246 us (81%)
  matrix products  25.1 us (8%)
  local copies, waits for them, and re-layouts  18.9 us (6%)
  between operations  13.1 us (4%)
    psum x1, waiting for transfers between devices, per_device(): lax.psum(up_part.astype(jnp.bfloat16), 'col').astype(jnp.float32)  198 us
    reduce_scatter x1, waiting for transfers between devices, per_device(): lax.psum_scatter(jnp.dot(hidden, kept_down, preferred_element_type=jnp.fl...  32.1 us
    unnamed x14, local copies, waits for them, and re-layouts  15.6 us
    all_gather x1, waiting for transfers between devices, per_device(): gathered = lax.all_gather(tokens, 'row', axis=0, tiled=True)  14.7 us
    dot_general x1, matrix products, per_device(): jnp.dot(hidden, kept_down, preferred_element_type=jnp.float32)  11.6 us
    dot_general x1, matrix products, per_device(): gate_part = jnp.dot(gathered, kept_gate, preferred_element_type=jnp.float32)  7.45 us
    dot_general x1, matrix products, per_device(): up_part = jnp.dot(gathered, kept_up, preferred_element_type=jnp.float32)  6.08 us
  transfers between devices with their start and end apart: 3, of which 3 were waited for; matrix products, arithmetic and copies ran while one was open for 4% of the time, Pallas kernels for 0%

commit v1 on v0

--- a/solution.py
+++ b/solution.py
@@ -2,6 +2,38 @@
 import jax.numpy as jnp
 from jax import lax
 from jax.sharding import PartitionSpec as P
+
+
+def find_roads(work_x):
+    oldest, u1, block_last = (jax.lax.axis_size("row"), jax.lax.axis_index("row"), work_x.shape[0])
+    panels = []
+    for ix, k0 in enumerate(work_x.shape):
+        panels.append(k0 * oldest if ix == 0 else k0)
+    y2 = lax.dynamic_update_slice_in_dim(
+        jnp.zeros(panels, work_x.dtype), work_x, u1 * block_last, axis=0
+    )
+    j0 = 1
+    block_out = all_values = work_x
+    while j0 < oldest // 2 + 1:
+        rows = []
+        ix = 0
+        while ix < oldest:
+            rows.append((ix, (ix + 1) % oldest))
+            ix = ix + 1
+        block_out = jax.lax.ppermute(block_out, "row", rows)
+        y2 = lax.dynamic_update_slice_in_dim(y2, block_out, (u1 - j0) % oldest * block_last, axis=0)
+        if 2 * j0 < oldest:
+            shelf = []
+            ix = 0
+            while ix < oldest:
+                shelf.append((ix, (ix - 1) % oldest))
+                ix += 1
+            all_values = jax.lax.ppermute(all_values, "row", shelf)
+            y2 = lax.dynamic_update_slice_in_dim(
+                y2, all_values, (u1 + j0) % oldest * block_last, axis=0
+            )
+        j0 += 1
+    return y2
 
 
 def expand(weight, block_mask):
@@ -16,7 +48,7 @@
     kept_gate = expand(gate_weight, gate_mask)
     kept_up = expand(up_weight, up_mask)
     kept_down = expand(down_weight, down_mask)
-    gathered = lax.all_gather(tokens, "row", axis=0, tiled=True)
+    gathered = find_roads(tokens)
     gate_part = jnp.dot(gathered, kept_gate, preferred_element_type=jnp.float32)
     up_part = jnp.dot(gathered, kept_up, preferred_element_type=jnp.float32)
     gate_sum, up_sum = (

time: 304 us -> 305 us (level)
  starting transfers between devices: 0.08 us -> 8.91 us
  waiting for transfers between devices: 246 us -> 241 us
  matrix products: 25.1 us -> 21.9 us
    all_gather x1 -> x0, waiting for transfers between devices: 14.7 us -> none  [per_device(): gathered = lax.all_gather(tokens, 'row', axis=0, tiled=True)]
    ppermute x0 -> x7, waiting for transfers between devices: none -> 10.8 us  [the longest x4 10.8 us: find_roads(): block_out = jax.lax.ppermute(block_out, 'row', rows)]
    ppermute x0 -> x7, starting transfers between devices: none -> 8.87 us  [the longest x3 8.84 us: find_roads(): all_values = jax.lax.ppermute(all_values, 'row', shelf)]
  transfers between devices with their start and end apart: 3 -> 9, of which waited for: 3 -> 5; matrix products, arithmetic and copies ran while one was open for 4% -> 4% of each run, Pallas kernels for 0% -> 0%
where the time goes in v1:
time: 305 us; the launch traced here: 304 us
  waiting for transfers between devices  241 us (79%)
  matrix products  21.9 us (7%)
  local copies, waits for them, and re-layouts  18.1 us (6%)
  between operations  13.5 us (4%)
  starting transfers between devices  8.91 us (3%)
    psum x1, waiting for transfers between devices, per_device(): lax.psum(up_part.astype(jnp.bfloat16), 'col').astype(jnp.float32)  198 us
    reduce_scatter x1, waiting for transfers between devices, per_device(): lax.psum_scatter(jnp.dot(hidden, kept_down, preferred_element_type=jnp.fl...  32.1 us
    unnamed x14, local copies, waits for them, and re-layouts  14.6 us
    ppermute x4, waiting for transfers between devices, find_roads(): block_out = jax.lax.ppermute(block_out, 'row', rows)  10.8 us
    dot_general x1, matrix products, per_device(): jnp.dot(hidden, kept_down, preferred_element_type=jnp.float32)  9.69 us
    ppermute x3, starting transfers between devices, find_roads(): all_values = jax.lax.ppermute(all_values, 'row', shelf)  8.84 us
    dot_general x1, matrix products, per_device(): up_part = jnp.dot(gathered, kept_up, preferred_element_type=jnp.float32)  6.12 us
  transfers between devices with their start and end apart: 9, of which 5 were waited for; matrix products, arithmetic and copies ran while one was open for 4% of the time, Pallas kernels for 0%

profile of v1, /device:TPU:0, one launch (start us, length us, event | category | flops | bytes accessed | tf_op | source)
XLA Modules:
  0.0 304.3 jit_solution(14780556473474078986)
XLA Ops:
  6.5 0.0 all-reduce.3.cloned.1.call-start
  6.5 0.0 collective-permute-start
  6.5 3.0 collective-permute-start.1
  9.5 0.7 convert_element_type.30
  10.2 0.1 copy.11
  10.3 0.0 copy-start.3
  10.3 5.9 %copy.12 = bf16[512,3584]{0,1:T(8,128)(2,1)} copy(bf16[512,3584]{1,0:T(8,128)(2,1)} %param.9) | data formatting | bytes 7340032 | tf_op args[2]
  16.2 0.0 copy-done.3
  16.2 0.1 copy.9
  16.4 0.0 copy-start.2
  16.4 6.0 %copy.10 = bf16[512,3584]{0,1:T(8,128)(2,1)} copy(bf16[512,3584]{1,0:T(8,128)(2,1)} %param.8) | data formatting | bytes 7340032 | tf_op args[1]
  22.3 0.0 copy-start.1
  22.3 0.1 broadcast_in_dim.2
  22.4 0.0 copy-done.2
  22.4 0.0 collective-permute-done
  22.5 0.0 collective-permute-start.2
  22.5 0.0 collective-permute-done.1
  22.5 2.9 collective-permute-start.3
  25.5 2.6 collective-permute-done.2
  28.1 0.0 collective-permute-start.4
  28.1 0.0 collective-permute-done.3
  28.1 3.0 collective-permute-start.5
  31.1 2.6 collective-permute-done.4
  33.7 0.0 collective-permute-start.6
  33.7 0.0 collective-permute-done.5
  33.7 5.5 %collective-permute-done.6 = bf16[128,512]{1,0:T(8,128)(2,1)S(1)} collective-permute-done((bf16[128,512]{1,0:T(8,128)(2,1)S(1)}, bf16[128,512]{1,0:T(8,128)(2,1)S(1)}, u32[]{:S(2)}, u32[]{:S(2)}) %collective-permute-start.6) | collective-permute-done | bytes 131104 | tf_op jit(solution)/shard_map/ppermute | solution.py:23
  39.3 1.0 mul.76
  40.3 0.0 copy-done.1
  40.3 6.1 %convolution_convert_fusion = bf16[1024,3584]{1,0:T(8,128)(2,1)} fusion(bf16[1024,512]{1,0:T(8,128)(2,1)S(1)} %constant_dynamic-update-slice_fusion, bf16[512,3584]{0,1:T(8,128)(2,1)S(1)} %copy-done.1, bf16[448,8,4,128]{3,2,1,0:T(4,128)(2,1)S(1)} %bitcast.25), kind=kOutput, calls=%fused_computation.7 | convolution fusion | flops 3763601408 | bytes 15728640 | tf_op jit(solution)/shard_map/dot_general | solution.py:53
  46.4 0.0 copy-start
  46.4 1.0 mul.72
  47.5 1.0 copy-done
  48.5 6.1 %convolution_convert_fusion.1 = bf16[1024,3584]{1,0:T(8,128)(2,1)} fusion(bf16[1024,512]{1,0:T(8,128)(2,1)S(1)} %constant_dynamic-update-slice_fusion, bf16[512,3584]{0,1:T(8,128)(2,1)S(1)} %copy-done, bf16[448,8,4,128]{3,2,1,0:T(4,128)(2,1)S(1)} %bitcast.23), kind=kOutput, calls=%fused_computation.8 | convolution fusion | flops 3763601408 | bytes 15728640 | tf_op jit(solution)/shard_map/dot_general | solution.py:52
  54.6 0.0 copy-start.4
  54.6 0.0 all-reduce.3.cloned.1.call-update
  54.6 0.0 reduce-scatter.2.cloned.1.call-start
  54.6 0.6 copy-done.4
  55.2 0.1 copy.13
  55.4 198.3 %all-reduce.3.cloned.1.call-done = (bf16[1024,3584]{1,0:T(8,128)(2,1)}, bf16[1024,3584]{1,0:T(8,128)(2,1)}) async-done(((bf16[1024,3584]{1,0:T(8,128)(2,1)}, bf16[1024,3584]{1,0:T(8,128)(2,1)}), (bf16[1024,3584]{1,0:T(8,128)(2,1)}, bf16[1024,3584]{1,0:T(8,128)(2,1)})) %all-reduce.3.cloned.1.call-update) | async-done | bytes 14680080 | tf_op jit(solution)/shard_map/psum | solution.py:56
  253.7 0.0 copy-start.5
  253.7 1.0 mul.80
  254.7 1.0 copy-done.5
  255.7 9.7 %fusion.10 = bf16[1024,512]{1,0:T(8,128)(2,1)} fusion(bf16[3584,512]{1,0:T(8,128)(2,1)S(1)} %copy-done.5, bf16[448,8,4,128]{3,2,1,0:T(4,128)(2,1)S(1)} %bitcast.24, bf16[1024,3584]{1,0:T(8,128)(2,1)} %get-tuple-element.5, bf16[1024,3584]{1,0:T(8,128)(2,1)} %get-tuple-element.6), kind=kOutput, calls=%fused_computation.16 | convolution fusion | flops 3789815808 | bytes 23068672 | tf_op jit(solution)/shard_map/dot_general | solution.py:60
  265.4 0.0 reduce-scatter.2.cloned.1.call-update
  265.4 32.1 %reduce-scatter.2.cloned.1.call-done = bf16[128,512]{1,0:T(8,128)(2,1)} async-done(((bf16[1024,512]{1,0:T(8,128)(2,1)}), bf16[128,512]{1,0:T(8,128)(2,1)}) %reduce-scatter.2.cloned.1.call-update) | async-done | bytes 131088 | tf_op jit(solution)/shard_map/reduce_scatter | solution.py:59
  (10 shorter events, 0.1 us)
Async XLA Ops:
  6.5 247.1 %all-reduce.3.cloned.1.call-start = ((), (), s32[]{:S(2)}) async-start(), calls=%async_computation.2 | async-start | bytes 29360128 | tf_op jit(solution)/shard_map/psum | solution.py:56
  6.5 15.9 %collective-permute-start = (bf16[128,512]{1,0:T(8,128)(2,1)}, bf16[128,512]{1,0:T(8,128)(2,1)S(1)}, u32[]{:S(2)}, u32[]{:S(2)}) collective-permute-start(bf16[128,512]{1,0:T(8,128)(2,1)} %param.7), channel_id=1, source_target_pairs={{0,16},{16,32},{32,48},{48,64},{64,80},{80,96},{96,112},{112,0},{1... | collective-permute-start | bytes 393224 | tf_op jit(solution)/shard_map/ppermute | solution.py:23
  6.5 15.9 %collective-permute-start.1 = (bf16[128,512]{1,0:T(8,128)(2,1)}, bf16[128,512]{1,0:T(8,128)(2,1)S(1)}, u32[]{:S(2)}, u32[]{:S(2)}) collective-permute-start(bf16[128,512]{1,0:T(8,128)(2,1)} %param.7), channel_id=1, source_target_pairs={{0,112},{16,0},{32,16},{48,32},{64,48},{80,64},{96,80},{112,96},{1... | collective-permute-start | bytes 393224 | tf_op jit(solution)/shard_map/ppermute | solution.py:31
  10.3 5.9 %copy-start.3 = (s32[4,28]{1,0:T(4,128)S(1)}, s32[4,28]{1,0:T(4,128)}, u32[]{:S(2)}) copy-start(s32[4,28]{1,0:T(4,128)} %param.11) | copy-start | bytes 1348
  16.4 6.1 %copy-start.2 = (bf16[128,512]{1,0:T(8,128)(2,1)S(1)}, bf16[128,512]{1,0:T(8,128)(2,1)}, u32[]{:S(2)}) copy-start(bf16[128,512]{1,0:T(8,128)(2,1)} %param.7) | copy-start | bytes 393220
  22.3 18.0 %copy-start.1 = (bf16[512,3584]{0,1:T(8,128)(2,1)S(1)}, bf16[512,3584]{0,1:T(8,128)(2,1)}, u32[]{:S(2)}) copy-start(bf16[512,3584]{0,1:T(8,128)(2,1)} %copy.12) | copy-start | bytes 11010052
  22.5 5.6 %collective-permute-start.2 = (bf16[128,512]{1,0:T(8,128)(2,1)S(1)}, bf16[128,512]{1,0:T(8,128)(2,1)S(1)}, u32[]{:S(2)}, u32[]{:S(2)}) collective-permute-start(bf16[128,512]{1,0:T(8,128)(2,1)S(1)} %collective-permute-done), channel_id=1, source_target_pairs={{0,16},{16,32},{32,48},{48,64},{64,80},{80,96},{96,112},{112,0},{1... | collective-permute-start | bytes 393224 | tf_op jit(solution)/shard_map/ppermute | solution.py:23
  22.5 5.6 %collective-permute-start.3 = (bf16[128,512]{1,0:T(8,128)(2,1)S(1)}, bf16[128,512]{1,0:T(8,128)(2,1)S(1)}, u32[]{:S(2)}, u32[]{:S(2)}) collective-permute-start(bf16[128,512]{1,0:T(8,128)(2,1)S(1)} %collective-permute-done.1), channel_id=1, source_target_pairs={{0,112},{16,0},{32,16},{48,32},{64,48},{80,64},{96,80},{112,96},{1... | collective-permute-start | bytes 393224 | tf_op jit(solution)/shard_map/ppermute | solution.py:31
  28.1 5.6 %collective-permute-start.4 = (bf16[128,512]{1,0:T(8,128)(2,1)S(1)}, bf16[128,512]{1,0:T(8,128)(2,1)S(1)}, u32[]{:S(2)}, u32[]{:S(2)}) collective-permute-start(bf16[128,512]{1,0:T(8,128)(2,1)S(1)} %collective-permute-done.2), channel_id=1, source_target_pairs={{0,16},{16,32},{32,48},{48,64},{64,80},{80,96},{96,112},{112,0},{1... | collective-permute-start | bytes 393224 | tf_op jit(solution)/shard_map/ppermute | solution.py:23
  28.1 5.6 %collective-permute-start.5 = (bf16[128,512]{1,0:T(8,128)(2,1)S(1)}, bf16[128,512]{1,0:T(8,128)(2,1)S(1)}, u32[]{:S(2)}, u32[]{:S(2)}) collective-permute-start(bf16[128,512]{1,0:T(8,128)(2,1)S(1)} %collective-permute-done.3), channel_id=1, source_target_pairs={{0,112},{16,0},{32,16},{48,32},{64,48},{80,64},{96,80},{112,96},{1... | collective-permute-start | bytes 393224 | tf_op jit(solution)/shard_map/ppermute | solution.py:31
  33.7 5.6 %collective-permute-start.6 = (bf16[128,512]{1,0:T(8,128)(2,1)S(1)}, bf16[128,512]{1,0:T(8,128)(2,1)S(1)}, u32[]{:S(2)}, u32[]{:S(2)}) collective-permute-start(bf16[128,512]{1,0:T(8,128)(2,1)S(1)} %collective-permute-done.4), channel_id=1, source_target_pairs={{0,16},{16,32},{32,48},{48,64},{64,80},{80,96},{96,112},{112,0},{1... | collective-permute-start | bytes 393224 | tf_op jit(solution)/shard_map/ppermute | solution.py:23
  46.4 2.0 copy-start
  54.6 0.7 copy-start.4
  54.6 242.9 %reduce-scatter.2.cloned.1.call-start = ((), (), s32[]{:S(2)}) async-start(), calls=%async_computation.1 | async-start | bytes 1179648 | tf_op jit(solution)/shard_map/reduce_scatter | solution.py:59
  253.7 2.0 copy-start.5
Sparse Core Ops, SparseCore 0:
  54.7 198.9 all-reduce.2
  265.5 31.8 reduce-scatter.1
